TPU v7x, 256 devices: a whole 4x4x8 slice. The times are simulated.
256 devices in a mesh: grp: 4 (over y), seq: 16 (over z, core), head: 4 (over x).
Axes of the slice: x: 4, y: 4, z: 8, core: 2. Of those that a mesh axis runs over, the one named last changes fastest.
Arguments:
- keys: bfloat16 [32, 8192, 1536], P('grp', 'seq', 'head'), may hold values from -6 to 6
- values: bfloat16 [32, 8192, 1536], P('grp', 'seq', 'head'), may hold values from -6 to 6
- log_forget: float32 [32, 24, 8192], P('grp', 'head', 'seq'), may hold values from -0.6 to 0, as said below
- keep: int32 [32, 8192], P('grp', 'seq'), may hold values from 0 to 1, as said below
- merge_weight: float32 [32, 8192], P('grp', 'seq'), may hold values from 0.1 to 10
- lengths: int32 [32], P('grp'), may hold values from 64 to 8192, as said below
- route: int32 [32], P('grp'), may hold values from 0 to 31, as said below
- fresh: bfloat16 [3, 32, 1536], P(None, 'grp', 'head'), may hold values from -7.5 to 7.5
- new_forget: bfloat16 [32, 24], P('grp', 'head'), may hold values from -1 to -0.049804688
- out_weight: bfloat16 [1536, 1536], P('head', 'seq'), may hold values from -0.15625 to 0.15625
Outputs:
- compact_keys: bfloat16 [32, 4096, 1536], P('grp', 'seq', 'head')
- compact_values: bfloat16 [32, 4096, 1536], P('grp', 'seq', 'head')
- compact_decay: float32 [32, 24, 4096], P('grp', 'head', 'seq')
- layer_out: bfloat16 [32, 1536], P('grp', 'seq')
Inputs may be any that keep to these rules, and one draw needn't show every extreme that they name: `keep`: within every aligned block of 64 positions of a request, between 16 and 31 entries are 1, and some block has exactly 31. `lengths`: multiples of 64; the first request of every 8 in order has 8192. `route`: A permutation of the requests. `log_forget`: Negative.
All inputs are finite; a program needn't handle non-finite values.
Results may differ from a plain program's by a relative error of at most 0.0085.
Values may be sent and summed in bfloat16 or wider, within the bound.
A program may use at most 64 MiB of HBM per device.

v0:
```python
import jax
import jax.numpy as jnp
from jax import lax
from jax.sharding import PartitionSpec as P

BLOCK = 64
SLOTS = 32


EMPTY_LOG = -10000.0


def carried_in(value, axis, join, neutral):
    count, mine = (lax.axis_size(axis), lax.axis_index(axis))
    pieces = lax.all_gather(value, axis)
    pieces = pieces[::-1]
    mine = count - 1 - mine
    so_far = jnp.full_like(value, 0) + jnp.asarray(neutral, value.dtype)

    def turn(position, so_far):
        longer = join(so_far, pieces[position])
        return jnp.where(position < mine, longer, so_far)

    return lax.fori_loop(0, count - 1, turn, so_far)


def merged(value, axis, join):
    pieces = jax.tree.map(lambda part: lax.all_gather(part, axis), value)
    head = jax.tree.map(lambda part: part[0], pieces)
    tail = jax.tree.map(lambda part: part[1:], pieces)
    so_far, _ = lax.scan(lambda so_far, section: (join(so_far, section), None), head, tail)
    return so_far


def add_totals(earlier, later):
    return earlier + later


def merge_parts(first, second):
    top_one, sum_one, acc_one = first
    top_two, sum_two, acc_two = second
    joint = jnp.maximum(top_one, top_two)
    scale_one = jnp.exp(top_one - joint)
    scale_two = jnp.exp(top_two - joint)
    return (
        joint,
        sum_one * scale_one + sum_two * scale_two,
        acc_one * scale_one[..., None] + acc_two * scale_two[..., None],
    )


def shards(
    keys, values, log_forget, keep, merge_weight, lengths, route, fresh, new_forget, out_weight
):
    req_dev, pos_dev, width_dev = keys.shape
    heads_dev = log_forget.shape[1]
    head_size = width_dev // heads_dev
    blocks_dev = pos_dev // BLOCK
    rows_dev = blocks_dev * SLOTS
    shard = lax.axis_index("seq")
    position = shard * pos_dev + jnp.arange(pos_dev, dtype=jnp.int32)
    live = position[None, :] < lengths[:, None]
    forget = jnp.where(live[:, None, :], log_forget, 0.0)
    own_total = jnp.sum(forget, axis=2)
    inner = own_total[:, :, None] - jnp.cumsum(forget, axis=2)
    later_sum = carried_in(own_total, "seq", add_totals, jnp.zeros_like(own_total))
    log_decay = inner + later_sum[:, :, None]
    flags = keep.reshape(req_dev, blocks_dev, BLOCK)
    rank = jnp.cumsum(flags, axis=2) - 1
    slot_ids = jnp.arange(SLOTS - 1, dtype=jnp.int32)
    block_start = shard * pos_dev + jnp.arange(blocks_dev, dtype=jnp.int32) * BLOCK
    block_live = (block_start[None, :] < lengths[:, None]).astype(jnp.float32)
    chosen = (
        (flags[:, :, None, :] == 1) & (rank[:, :, None, :] == slot_ids[None, None, :, None])
    ).astype(jnp.float32)
    chosen = chosen * block_live[:, :, None, None]
    dropped = flags == 0
    weighted = jnp.where(dropped, merge_weight.reshape(req_dev, blocks_dev, BLOCK), 0.0)
    share = (
        (weighted / jnp.sum(weighted, axis=2, keepdims=True))
        .astype(jnp.bfloat16)
        .astype(jnp.float32)
    )
    merged_row = (share * block_live[:, :, None])[:, :, None, :]
    select = jnp.concatenate([chosen, merged_row], axis=2).astype(jnp.bfloat16)
    key_blocks = keys.reshape(req_dev, blocks_dev, BLOCK, width_dev)
    value_blocks = values.reshape(req_dev, blocks_dev, BLOCK, width_dev)
    packed_keys = (
        jnp.einsum("rbej,rbjc->rbec", select, key_blocks, preferred_element_type=jnp.float32)
        .astype(jnp.bfloat16)
        .reshape(req_dev, rows_dev, width_dev)
    )
    packed_values = (
        jnp.einsum("rbej,rbjc->rbec", select, value_blocks, preferred_element_type=jnp.float32)
        .astype(jnp.bfloat16)
        .reshape(req_dev, rows_dev, width_dev)
    )
    decay_blocks = log_decay.reshape(req_dev, heads_dev, blocks_dev, BLOCK)
    kept_log = jnp.einsum("rbej,rhbj->rhbe", chosen, decay_blocks, precision=lax.Precision.HIGHEST)
    filled = jnp.sum(chosen, axis=3)
    kept_log = kept_log + (1.0 - filled)[:, None, :, :] * EMPTY_LOG
    drop_mask = dropped[:, None, :, :]
    drop_peak = jnp.max(jnp.where(drop_mask, decay_blocks, -jnp.inf), axis=3)
    spread = jnp.where(drop_mask, jnp.exp(decay_blocks - drop_peak[..., None]), 0.0)
    merged_log = drop_peak + jnp.log(jnp.sum(share[:, None, :, :] * spread, axis=3))
    merged_log = jnp.where(block_live[:, None, :] > 0, merged_log, EMPTY_LOG)
    slot_log = jnp.concatenate([kept_log, merged_log[..., None]], axis=3).reshape(
        req_dev, heads_dev, rows_dev
    )
    compact_decay = jnp.exp(slot_log)
    dealt_keys, dealt_values = (
        lax.all_to_all(packed_keys, "seq", split_axis=1, concat_axis=1, tiled=True),
        lax.all_to_all(packed_values, "seq", split_axis=1, concat_axis=1, tiled=True),
    )
    arrived, arrived_forget = (
        lax.all_gather(fresh, "grp", axis=1, tiled=True),
        lax.all_gather(new_forget, "grp", axis=0, tiled=True),
    )
    picked = jnp.take(arrived, route, axis=1)
    new_log = jnp.take(arrived_forget, route, axis=0).astype(jnp.float32)
    query = picked[0].reshape(req_dev, heads_dev, head_size)
    own_key = picked[1].reshape(req_dev, heads_dev, head_size)
    own_value = picked[2].reshape(req_dev, heads_dev, head_size).astype(jnp.float32)
    scale = head_size ** (-0.5)
    key_rows = packed_keys.reshape(req_dev, rows_dev, heads_dev, head_size)
    value_rows = packed_values.reshape(req_dev, rows_dev, heads_dev, head_size)
    scores = (
        jnp.einsum("rhd,rnhd->rhn", query, key_rows, preferred_element_type=jnp.float32) * scale
        + slot_log
    )
    local_top = jnp.max(scores, axis=2)
    weights = jnp.exp(scores - local_top[..., None]).astype(jnp.bfloat16)
    local_sum = jnp.sum(weights.astype(jnp.float32), axis=2)
    local_acc = jnp.einsum("rhn,rnhd->rhd", weights, value_rows, preferred_element_type=jnp.float32)
    top, total_sum, total_acc = merged((local_top, local_sum, local_acc), "seq", merge_parts)
    own_score = jnp.sum(query.astype(jnp.float32) * own_key.astype(jnp.float32), axis=2) * scale
    cache_top = top + new_log
    joint = jnp.maximum(cache_top, own_score)
    cache_scale = jnp.exp(cache_top - joint)
    self_weight = jnp.exp(own_score - joint)
    attended = (cache_scale[..., None] * total_acc + self_weight[..., None] * own_value) / (
        cache_scale * total_sum + self_weight
    )[..., None]
    attended = attended.reshape(req_dev, width_dev).astype(jnp.bfloat16)
    partial_out = jnp.dot(attended, out_weight, preferred_element_type=jnp.float32)
    layer_out = lax.psum(partial_out, "head").astype(jnp.bfloat16)
    return (dealt_keys, dealt_values, compact_decay, layer_out)


def solution(mesh):
    return jax.shard_map(
        shards,
        mesh=mesh,
        in_specs=(
            P("grp", "seq", "head"),
            P("grp", "seq", "head"),
            P("grp", "head", "seq"),
            P("grp", "seq"),
            P("grp", "seq"),
            P("grp"),
            P("grp"),
            P(None, "grp", "head"),
            P("grp", "head"),
            P("head", "seq"),
        ),
        out_specs=(
            P("grp", "seq", "head"),
            P("grp", "seq", "head"),
            P("grp", "head", "seq"),
            P("grp", "seq"),
        ),
        check_vma=False,
    )
```

profile of v0, /device:TPU:1, one launch (start us, length us, event | category | flops | bytes accessed | tf_op | source)
XLA Modules:
  0.0 210.6 jit_solution(9465967890961578611)
XLA Ops:
  0.6 0.9 broadcast_in_dim_reshape.3
  3.3 1.8 reduce_window_sum.24
  5.1 1.3 broadcast_compare_fusion.3
  8.2 1.1 copy-done.1
  9.4 2.1 copy.80
  11.4 10.0 %all-to-all-start.1 = ((bf16[8,256,384]{2,0,1:T(8,128)(2,1)}), bf16[8,256,384]{2,0,1:T(8,128)(2,1)}, u32[]{:S(2)}, u32[]{:S(2)}) async-start(bf16[8,256,384]{2,0,1:T(8,128)(2,1)} %copy.80), calls=%async_computation.1 | async-start | bytes 3145728 | tf_op jit(solution)/shard_map/all_to_all | solution.py:113
  22.2 6.8 %reduce-window.6 = f32[8,6,4,128]{3,0,1,2:T(8,128)S(1)} reduce-window(f32[8,6,4,128]{3,0,1,2:T(8,128)S(1)} %copy.82, f32[]{:T(128)} %constant.91.clone.1), window={size=1x1x1x128 pad=0_0x0_0x0_0x127_0}, to_apply=%region_3.4 | reduce-window | flops 3121152 | bytes 196612 | tf_op jit(solution)/shard_map/reduce-window
  29.1 1.8 select_reduce_fusion
  30.9 5.9 %reshape_reshape.7 = bf16[8,256,6,64]{3,2,1,0:T(8,128)(2,1)} reshape(bf16[8,8,32,384]{3,2,1,0:T(8,128)(2,1)} %copy-done.1) | data formatting | bytes 3145728 | tf_op jit(solution)/shard_map/reshape;reshape | solution.py:126
  36.9 32.9 %all-gather = f32[128,6]{1,0:T(8,128)S(1)} all-gather(f32[8,6]{1,0:T(8,128)S(1)} %copy.81), channel_id=2, replica_groups=mesh['grp'=4,'seq'=16,'head'=4] {'seq'}, dimensions={0}, use_global_device_ids=true | all-gather | bytes 3264 | tf_op jit(solution)/shard_map/all_gather | solution.py:15
  70.0 1.5 while.29
  72.0 0.8 fusion.25
  72.9 1.0 select_reduce_fusion.1
  75.8 2.8 %fusion.13 = f32[8,6,8,31]{3,1,2,0:T(8,128)S(1)} fusion(f32[8,8]{1,0:T(8,128)S(1)} %get-tuple-element.223, s32[8,8,64]{2,1,0:T(8,128)} %copy-done.8, pred[8,8,64]{2,1,0:T(8,128)(4,1)} %copy-done.14, f32[8,6,8,64]{3,2,1,0:T(8,128)} %copy-done.5, f32[8,8,31]{2,1,0:T(8,128)S(1)} %subtract_multiply_fusion), kind=kOutput, calls=%fused_computation.25 | convolution fusion | flops 9535104 | bytes 174592 | tf_op jit(solution)/shard_map/rbej,rhbj->rhbe/dot_general | solution.py:99
  78.6 0.8 broadcast_select_fusion
  79.8 3.9 %convolution_convert_fusion.1 = bf16[8,8,32,384]{3,2,1,0:T(8,128)(2,1)} fusion(bf16[8,8,64,384]{3,2,1,0:T(8,128)(2,1)} %bitcast.75, bf16[8,8,1,64]{3,2,1,0:T(2,128)(2,1)S(1)} %copy-done.7, bf16[8,8,31,64]{3,2,1,0:T(8,128)(2,1)} %copy-done.2), kind=kOutput, calls=%fused_computation.23 | convolution fusion | flops 101974016 | bytes 4980736 | tf_op jit(solution)/shard_map/rbej,rbjc->rbec/dot_general | solution.py:89
  83.7 5.9 %reshape_reshape.6 = bf16[8,256,6,64]{3,2,1,0:T(8,128)(2,1)} reshape(bf16[8,8,32,384]{3,2,1,0:T(8,128)(2,1)} %convolution_convert_fusion.1) | data formatting | bytes 3145728 | tf_op jit(solution)/shard_map/reshape;reshape | solution.py:125
  89.6 9.9 %all_gather.32 = bf16[3,32,384]{2,1,0:T(8,128)(2,1)S(1)} all-gather(bf16[3,8,384]{2,1,0:T(8,128)(2,1)S(1)} %copy-done.18), channel_id=1, replica_groups=mesh['grp'=4,'seq'=16,'head'=4] {'grp'}, dimensions={1}, use_global_device_ids=true | all-gather | bytes 92160 | tf_op jit(solution)/shard_map/all_gather | solution.py:116
  101.6 3.1 %fusion.6 = f32[8,6,1,256]{3,2,1,0:T(1,128)S(1)} fusion(bf16[8,6,64,1]{2,3,1,0:T(2,128)(2,1)S(1)} %reshape.314, bf16[8,256,6,64]{3,2,1,0:T(8,128)(2,1)} %reshape_reshape.6), kind=kOutput, calls=%fused_computation.16 | convolution fusion | flops 1572864 | bytes 1628160 | tf_op jit(solution)/shard_map/rhd,rnhd->rhn/dot_general | solution.py:128
  105.6 2.7 %fusion.4 = f32[8,6,1,64]{3,2,1,0:T(1,128)S(1)} fusion(bf16[8,256,6,64]{3,2,1,0:T(8,128)(2,1)} %reshape_reshape.7, bf16[8,6,256,1]{2,0,1,3:T(8,128)(2,1)S(1)} %bitcast.80), kind=kOutput, calls=%fused_computation.14 | convolution fusion | flops 1572864 | bytes 1609728 | tf_op jit(solution)/shard_map/rhn,rnhd->rhd/dot_general | solution.py:134
  108.3 18.1 %all-gather.3 = f32[128,6,64]{2,0,1:T(8,128)S(1)} all-gather(f32[8,6,64]{2,0,1:T(8,128)S(1)} %bitcast.78), channel_id=5, replica_groups=mesh['grp'=4,'seq'=16,'head'=4] {'seq'}, dimensions={0}, use_global_device_ids=true | all-gather | bytes 208896 | tf_op jit(solution)/shard_map/all_gather | solution.py:28
  127.3 17.0 %all-gather.2 = f32[128,6]{1,0:T(8,128)S(1)} all-gather(f32[8,6]{1,0:T(8,128)S(1)} %copy.95), channel_id=4, replica_groups=mesh['grp'=4,'seq'=16,'head'=4] {'seq'}, dimensions={0}, use_global_device_ids=true | all-gather | bytes 3264 | tf_op jit(solution)/shard_map/all_gather | solution.py:28
  144.3 14.8 %all-gather.1 = f32[128,6]{1,0:T(8,128)S(1)} all-gather(f32[8,6]{1,0:T(8,128)S(1)} %copy.94), channel_id=3, replica_groups=mesh['grp'=4,'seq'=16,'head'=4] {'seq'}, dimensions={0}, use_global_device_ids=true | all-gather | bytes 3264 | tf_op jit(solution)/shard_map/all_gather | solution.py:28
  159.1 3.5 %copy.79 = bf16[8,256,384]{2,0,1:T(8,128)(2,1)} copy(bf16[8,256,384]{2,1,0:T(8,128)(2,1)} %bitcast.73) | data formatting | bytes 3145728 | tf_op jit(solution)/shard_map/reshape | solution.py:91
  163.9 5.3 %all-to-all-start = ((bf16[8,256,384]{2,0,1:T(8,128)(2,1)}), bf16[8,256,384]{2,0,1:T(8,128)(2,1)}, u32[]{:S(2)}, u32[]{:S(2)}) async-start(bf16[8,256,384]{2,0,1:T(8,128)(2,1)} %copy.79), calls=%async_computation | async-start | bytes 3145728 | tf_op jit(solution)/shard_map/all_to_all | solution.py:112
  169.1 12.3 %while.28 = (s32[]{:T(128)}, f32[8,6]{1,0:T(8,128)S(1)}, f32[8,6]{1,0:T(8,128)S(1)}, f32[8,6,64]{2,1,0:T(8,128)S(1)}, f32[15,8,6]{2,1,0:T(8,128)}, /*index=5*/f3...) while((s32[]{:T(128)}, f32[8,6]{1,0:T(8,128)S(1)}, f32[8,6]{1,0:T(8,128)S(1)}, ...), condition=%wide.region_13.14_spmd, body=%wide.region_12.13_spmd.sunk | while | flops 9506 | bytes 63453 | solution.py:31
  182.2 0.9 fusion.29
  183.2 9.2 %all_gather.39 = bf16[32,6]{1,0:T(8,128)(2,1)S(1)} all-gather(bf16[8,6]{1,0:T(8,128)(2,1)} %param.22), channel_id=1, replica_groups=mesh['grp'=4,'seq'=16,'head'=4] {'grp'}, dimensions={0}, use_global_device_ids=true | all-gather | bytes 480 | tf_op jit(solution)/shard_map/all_gather | solution.py:117
  194.2 1.0 fusion.38
  195.2 9.8 %psum.7 = bf16[8,96]{1,0:T(8,128)(2,1)} all-reduce(f32[8,96]{1,0:T(8,128)S(1)} %fusion.38), channel_id=1, replica_groups=mesh['grp'=4,'seq'=16,'head'=4] {'head'}, use_global_device_ids=true, to_apply=%region_15.16 | all-reduce | flops 768 | bytes 4608 | tf_op jit(solution)/shard_map/psum | solution.py:146
  205.1 2.8 %copy.103 = bf16[8,256,384]{2,1,0:T(8,128)(2,1)} copy(bf16[8,256,384]{2,0,1:T(8,128)(2,1)} %all-to-all-done.1) | data formatting | bytes 3145728
  207.8 2.8 %copy.102 = bf16[8,256,384]{2,1,0:T(8,128)(2,1)} copy(bf16[8,256,384]{2,0,1:T(8,128)(2,1)} %all-to-all-done) | data formatting | bytes 3145728
  (202 shorter events, 28.5 us)
Async XLA Ops:
  0.6 6.3 %copy-start = (bf16[8,512,384]{2,1,0:T(8,128)(2,1)S(1)}, bf16[8,512,384]{2,1,0:T(8,128)(2,1)}, u32[]{:S(2)}) copy-start(bf16[8,512,384]{2,1,0:T(8,128)(2,1)} %param.15) | copy-start | bytes 9437188
  2.4 5.8 %copy-start.9 = (f32[8,8,64]{2,1,0:T(8,128)}, f32[8,8,64]{2,1,0:T(8,128)S(1)}, u32[]{:S(2)}) copy-start(f32[8,8,64]{2,1,0:T(8,128)S(1)} %reshape.266) | copy-start | bytes 49156
  3.2 5.0 %copy-start.14 = (pred[8,8,64]{2,1,0:T(8,128)(4,1)}, pred[8,8,64]{2,1,0:T(8,128)(4,1)S(1)}, u32[]{:S(2)}) copy-start(pred[8,8,64]{2,1,0:T(8,128)(4,1)S(1)} %broadcast_compare_fusion.1) | copy-start | bytes 12292
  3.2 4.9 %copy-start.16 = (f32[8,8]{1,0:T(8,128)}, f32[8,8]{1,0:T(8,128)S(1)}, u32[]{:S(2)}) copy-start(f32[8,8]{1,0:T(8,128)S(1)} %get-tuple-element.217) | copy-start | bytes 772
  5.0 6.4 %copy-start.8 = (s32[8,8,64]{2,1,0:T(8,128)}, s32[8,8,64]{2,1,0:T(8,128)S(1)}, u32[]{:S(2)}) copy-start(s32[8,8,64]{2,1,0:T(8,128)S(1)} %broadcast_add_fusion) | copy-start | bytes 49156
  6.7 0.8 copy-start.2
  6.9 1.3 copy-start.6
  8.2 1.1 copy-start.1
  9.4 12.1 %copy-start.22 = (s32[8]{0:T(128)S(1)}, s32[8]{0:T(128)}, u32[]{:S(2)}) copy-start(s32[8]{0:T(128)} %param.19) | copy-start | bytes 100
  9.4 12.2 %copy-start.13 = (f32[8,6,512]{2,0,1:T(8,128)S(1)}, f32[8,6,512]{2,0,1:T(8,128)}, u32[]{:S(2)}) copy-start(f32[8,6,512]{2,0,1:T(8,128)} %param.16) | copy-start | bytes 294916
  11.4 152.4 %all-to-all-start.1 = ((bf16[8,256,384]{2,0,1:T(8,128)(2,1)}), bf16[8,256,384]{2,0,1:T(8,128)(2,1)}, u32[]{:S(2)}, u32[]{:S(2)}) async-start(bf16[8,256,384]{2,0,1:T(8,128)(2,1)} %copy.80), calls=%async_computation.1 | async-start | bytes 3145728 | tf_op jit(solution)/shard_map/all_to_all | solution.py:113
  29.0 7.8 %copy-start.19 = (f32[8,6]{0,1:T(8,128)S(1)}, f32[8,6]{0,1:T(8,128)}, u32[]{:S(2)}) copy-start(f32[8,6]{0,1:T(8,128)} %get-tuple-element.220) | copy-start | bytes 580
  36.9 32.9 %copy-start.17 = (f32[8,6]{1,0:T(8,128)}, f32[8,6]{1,0:T(8,128)S(1)}, u32[]{:S(2)}) copy-start(f32[8,6]{1,0:T(8,128)S(1)} %copy.81) | copy-start | bytes 580
  71.7 8.1 %copy-start.7 = (bf16[8,8,1,64]{3,2,1,0:T(2,128)(2,1)S(1)}, bf16[8,8,1,64]{3,2,1,0:T(2,128)(2,1)}, u32[]{:S(2)}) copy-start(bf16[8,8,1,64]{3,2,1,0:T(2,128)(2,1)} %copy-done.6) | copy-start | bytes 24580
  73.9 0.7 copy-start.5
  83.7 5.9 %copy-start.18 = (bf16[3,8,384]{2,1,0:T(8,128)(2,1)S(1)}, bf16[3,8,384]{2,1,0:T(8,128)(2,1)}, u32[]{:S(2)}) copy-start(bf16[3,8,384]{2,1,0:T(8,128)(2,1)} %param.21) | copy-start | bytes 55300
  83.7 15.9 %copy-start.23 = (s32[8]{0:T(128)S(1)}, s32[8]{0:T(128)}, u32[]{:S(2)}) copy-start(s32[8]{0:T(128)} %param.20) | copy-start | bytes 100
  99.6 8.7 %copy-start.20 = (s32[1024]{0:T(1024)}, s32[1024]{0:T(1024)S(1)}, u32[]{:S(2)}) copy-start(s32[1024]{0:T(1024)S(1)} %pad_clamp_fusion) | copy-start | bytes 12292
  100.2 8.1 %copy-start.21 = (pred[8]{0:T(512)(128)(4,1)}, pred[8]{0:T(512)(128)(4,1)S(1)}, u32[]{:S(2)}) copy-start(pred[8]{0:T(512)(128)(4,1)S(1)} %compare_and_fusion) | copy-start | bytes 28
  100.3 0.6 copy-start.12
  100.9 0.6 copy-start.15
  126.5 0.7 copy-start.3
  127.3 36.5 %copy-start.4 = (f32[128,6,64]{2,0,1:T(8,128)S(1)}, f32[128,6,64]{2,0,1:T(8,128)}, u32[]{:S(2)}) copy-start(f32[128,6,64]{2,0,1:T(8,128)} %copy-done.3) | copy-start | bytes 589828
  144.3 18.9 %copy-start.10 = (f32[128,6]{1,0:T(8,128)}, f32[128,6]{1,0:T(8,128)S(1)}, u32[]{:S(2)}) copy-start(f32[128,6]{1,0:T(8,128)S(1)} %all-gather.2) | copy-start | bytes 9220
  159.0 4.7 %copy-start.11 = (f32[128,6]{1,0:T(8,128)}, f32[128,6]{1,0:T(8,128)S(1)}, u32[]{:S(2)}) copy-start(f32[128,6]{1,0:T(8,128)S(1)} %all-gather.1) | copy-start | bytes 9220
  163.8 5.3 %slice-start = ((f32[128,6]{1,0:T(8,128)}), f32[8,6]{1,0:T(8,128)S(1)}, s32[]{:S(2)}) async-start(f32[128,6]{1,0:T(8,128)} %copy-done.10), calls=%async_computation.2 | async-start | bytes 8192 | tf_op jit(solution)/shard_map/slice | solution.py:29
  163.8 5.3 %slice-start.1 = ((f32[128,6]{1,0:T(8,128)}), f32[8,6]{1,0:T(8,128)S(1)}, s32[]{:S(2)}) async-start(f32[128,6]{1,0:T(8,128)} %copy-done.11), calls=%async_computation.3 | async-start | bytes 8192 | tf_op jit(solution)/shard_map/slice | solution.py:29
  163.9 44.0 %all-to-all-start = ((bf16[8,256,384]{2,0,1:T(8,128)(2,1)}), bf16[8,256,384]{2,0,1:T(8,128)(2,1)}, u32[]{:S(2)}, u32[]{:S(2)}) async-start(bf16[8,256,384]{2,0,1:T(8,128)(2,1)} %copy.79), calls=%async_computation | async-start | bytes 3145728 | tf_op jit(solution)/shard_map/all_to_all | solution.py:112
where the time goes:
time: 214 us; the launch traced here: 211 us
  blocking collectives  112 us (52%)
  local copies, waits for them, and re-layouts  35.5 us (17%)
  other arithmetic  32.4 us (15%)
  starting transfers between devices  15.2 us (7%)
  matrix products  14.2 us (7%)
    all_gather x3, blocking collectives, merged(): pieces = jax.tree.map(lambda part: lax.all_gather(part, axis), value)  49.9 us
    all_gather x1, blocking collectives, carried_in(): pieces = lax.all_gather(value, axis)  32.9 us
    add x15, other arithmetic, merge_parts(): sum_one * scale_one + sum_two * scale_two  10.6 us
    all_to_all x1, starting transfers between devices, shards(): lax.all_to_all(packed_values, 'seq', split_axis=1, concat_axis=1, tiled=T...  9.98 us
    all_gather x1, blocking collectives, shards(): lax.all_gather(fresh, 'grp', axis=1, tiled=True)  9.9 us
    psum x1, blocking collectives, shards(): layer_out = lax.psum(partial_out, 'head').astype(jnp.bfloat16)  9.83 us
    unnamed x50, local copies, waits for them, and re-layouts  9.62 us
    all_gather x1, blocking collectives, shards(): lax.all_gather(new_forget, 'grp', axis=0, tiled=True)  9.24 us
  transfers between devices with their start and end apart: 2, of which 0 were waited for; matrix products, arithmetic and copies ran while one was open for 31% of the time, Pallas kernels for 0%

commit v1 on v0

v1 whole, which is shorter than its diff:
```python
import jax
import jax.numpy as jnp
from jax import lax
from jax.sharding import PartitionSpec as P

BLOCK = 64
SLOTS = 32


EMPTY_LOG = -10000.0
HIGHEST = lax.Precision.HIGHEST


def shards(
    keys, values, log_forget, keep, merge_weight, lengths, route, fresh, new_forget, out_weight
):
    f32, bf16 = jnp.float32, jnp.bfloat16
    req_dev, pos_dev, width_dev = keys.shape
    heads_dev = log_forget.shape[1]
    head_size = width_dev // heads_dev
    blocks_dev = pos_dev // BLOCK
    rows_dev = blocks_dev * SLOTS
    n_seq = lax.axis_size("seq")
    shard = lax.axis_index("seq")

    grp_req = fresh.shape[1]
    packed_fresh = jnp.concatenate(
        [fresh.transpose(1, 0, 2).reshape(grp_req, 3 * width_dev), new_forget], axis=1
    )
    arrived = lax.all_gather(packed_fresh, "grp", axis=0, tiled=True)
    picked = jnp.take(arrived, route, axis=0)
    query = picked[:, :width_dev]
    own_key = picked[:, width_dev : 2 * width_dev]
    own_value = picked[:, 2 * width_dev : 3 * width_dev].astype(f32)
    new_log = picked[:, 3 * width_dev :].astype(f32)

    position = shard * pos_dev + jnp.arange(pos_dev, dtype=jnp.int32)
    live = position[None, :] < lengths[:, None]
    forget = jnp.where(live[:, None, :], log_forget, 0.0)
    forget_blocks = forget.reshape(req_dev, heads_dev, blocks_dev, BLOCK)
    at = jnp.arange(BLOCK, dtype=jnp.int32)
    after = (at[:, None] > at[None, :]).astype(f32)
    within = jnp.einsum("rhbt,tp->rhbp", forget_blocks, after, precision=HIGHEST)
    block_total = jnp.sum(forget_blocks, axis=3)
    own_total = jnp.sum(block_total, axis=2)
    bt = jnp.arange(blocks_dev, dtype=jnp.int32)
    later_block = jnp.einsum(
        "rhb,bc->rhc", block_total, (bt[:, None] > bt[None, :]).astype(f32), precision=HIGHEST
    )
    totals = lax.all_gather(own_total, "seq")
    later_shard = jnp.sum(
        jnp.where((jnp.arange(n_seq) > shard)[:, None, None], totals, 0.0), axis=0
    )
    decay_blocks = within + later_block[..., None] + later_shard[:, :, None, None]

    flags = keep.reshape(req_dev, blocks_dev, BLOCK)
    upto = (at[:, None] <= at[None, :]).astype(bf16)
    rank = (
        jnp.einsum("rbt,tp->rbp", flags.astype(bf16), upto, preferred_element_type=f32).astype(
            jnp.int32
        )
        - 1
    )
    slot_ids = jnp.arange(SLOTS - 1, dtype=jnp.int32)
    block_start = shard * pos_dev + bt * BLOCK
    block_live = (block_start[None, :] < lengths[:, None]).astype(f32)
    chosen = (
        (flags[:, :, None, :] == 1) & (rank[:, :, None, :] == slot_ids[None, None, :, None])
    ).astype(f32)
    chosen = chosen * block_live[:, :, None, None]
    dropped = flags == 0
    weighted = jnp.where(dropped, merge_weight.reshape(req_dev, blocks_dev, BLOCK), 0.0)
    share = (
        (weighted / jnp.sum(weighted, axis=2, keepdims=True)).astype(bf16).astype(f32)
    )
    merged_row = (share * block_live[:, :, None])[:, :, None, :]
    select = jnp.concatenate([chosen, merged_row], axis=2).astype(bf16)
    key_blocks = keys.reshape(req_dev, blocks_dev, BLOCK, width_dev)
    value_blocks = values.reshape(req_dev, blocks_dev, BLOCK, width_dev)
    packed_keys = (
        jnp.einsum("rbej,rbjc->rbec", select, key_blocks, preferred_element_type=f32)
        .astype(bf16)
        .reshape(req_dev, rows_dev, width_dev)
    )
    packed_values = (
        jnp.einsum("rbej,rbjc->rbec", select, value_blocks, preferred_element_type=f32)
        .astype(bf16)
        .reshape(req_dev, rows_dev, width_dev)
    )
    dealt = lax.all_to_all(
        jnp.stack([packed_keys, packed_values]), "seq", split_axis=2, concat_axis=2, tiled=True
    )

    kept_log = jnp.einsum("rbej,rhbj->rhbe", chosen, decay_blocks, precision=HIGHEST)
    filled = jnp.sum(chosen, axis=3)
    kept_log = kept_log + (1.0 - filled)[:, None, :, :] * EMPTY_LOG
    drop_mask = dropped[:, None, :, :]
    drop_peak = jnp.max(jnp.where(drop_mask, decay_blocks, -jnp.inf), axis=3)
    spread = jnp.where(drop_mask, jnp.exp(decay_blocks - drop_peak[..., None]), 0.0)
    merged_log = drop_peak + jnp.log(jnp.sum(share[:, None, :, :] * spread, axis=3))
    merged_log = jnp.where(block_live[:, None, :] > 0, merged_log, EMPTY_LOG)
    slot_log = jnp.concatenate([kept_log, merged_log[..., None]], axis=3).reshape(
        req_dev, heads_dev, rows_dev
    )
    compact_decay = jnp.exp(slot_log)

    scale = head_size ** (-0.5)
    head_of = jnp.arange(width_dev, dtype=jnp.int32) // head_size
    onehot = head_of[:, None] == jnp.arange(heads_dev, dtype=jnp.int32)[None, :]
    query_blocks = jnp.where(onehot[None], query[:, :, None], jnp.zeros((), bf16))
    scores = (
        jnp.einsum("rnc,rch->rhn", packed_keys, query_blocks, preferred_element_type=f32) * scale
        + slot_log
    )
    local_top = jnp.max(scores, axis=2)
    weights = jnp.exp(scores - local_top[..., None]).astype(bf16)
    local_sum = jnp.sum(weights.astype(f32), axis=2)
    full_acc = jnp.einsum("rhn,rnc->rhc", weights, packed_values, preferred_element_type=f32)
    local_acc = jnp.sum(jnp.where(onehot.T[None], full_acc, 0.0), axis=1)
    stats = jnp.concatenate([local_top, local_sum, local_acc], axis=1)
    every = lax.all_gather(stats, "seq")
    tops = every[:, :, :heads_dev]
    sums = every[:, :, heads_dev : 2 * heads_dev]
    accs = every[:, :, 2 * heads_dev :]
    top = jnp.max(tops, axis=0)
    rescale = jnp.exp(tops - top[None])
    total_sum = jnp.sum(rescale * sums, axis=0)
    total_acc = jnp.sum(jnp.repeat(rescale, head_size, axis=2) * accs, axis=0)

    own_score = (
        jnp.sum(
            (query.astype(f32) * own_key.astype(f32)).reshape(req_dev, heads_dev, head_size),
            axis=2,
        )
        * scale
    )
    cache_top = top + new_log
    joint = jnp.maximum(cache_top, own_score)
    cache_scale = jnp.exp(cache_top - joint)
    self_weight = jnp.exp(own_score - joint)
    numer = (
        jnp.repeat(cache_scale, head_size, axis=1) * total_acc
        + jnp.repeat(self_weight, head_size, axis=1) * own_value
    )
    denom = jnp.repeat(cache_scale * total_sum + self_weight, head_size, axis=1)
    attended = (numer / denom).astype(bf16)
    partial_out = jnp.dot(attended, out_weight, preferred_element_type=f32)
    layer_out = lax.psum(partial_out, "head").astype(bf16)
    return (dealt[0], dealt[1], compact_decay, layer_out)


def solution(mesh):
    return jax.shard_map(
        shards,
        mesh=mesh,
        in_specs=(
            P("grp", "seq", "head"),
            P("grp", "seq", "head"),
            P("grp", "head", "seq"),
            P("grp", "seq"),
            P("grp", "seq"),
            P("grp"),
            P("grp"),
            P(None, "grp", "head"),
            P("grp", "head"),
            P("head", "seq"),
        ),
        out_specs=(
            P("grp", "seq", "head"),
            P("grp", "seq", "head"),
            P("grp", "head", "seq"),
            P("grp", "seq"),
        ),
        check_vma=False,
    )
```

time: 214 us -> 157 us (0.73)
  other arithmetic: 32.4 us -> 11.5 us
  local copies, waits for them, and re-layouts: 35.5 us -> 18.8 us
  blocking collectives: 112 us -> 105 us
  matrix products: 14.2 us -> 8.72 us
  starting transfers between devices: 15.2 us -> 10.1 us
    another operation x10 -> x2, local copies, waits for them, and re-layouts: 13.9 us -> 1.85 us  [shards(): jnp.stack([packed_keys, packed_values])]
    add x32 -> x2, other arithmetic: 12.7 us -> 0.7 us  [the longest x1 0.69 us: shards(): denom = jnp.repeat(cache_scale * total_sum + self_weight, head_size, axis=1)]
    another operation x5 -> x3, other arithmetic: 9.05 us -> 2.59 us  [the longest x1 2.11 us: shards(): jnp.stack([packed_keys, packed_values])]
    all_gather x6 -> x3, blocking collectives: 102 us -> 95.8 us  [the longest x1 70.1 us: shards(): totals = lax.all_gather(own_total, 'seq')]
    all_to_all x2 -> x1, starting transfers between devices: 15.2 us -> 10.1 us  [shards(): lax.all_to_all(jnp.stack([packed_keys, packed_values]), 'seq', split_axis...]
    unnamed x50 -> x40, local copies, waits for them, and re-layouts: 9.62 us -> 5.05 us
    dot_general x1, matrix products: 3.89 us -> 0.67 us  [shards(): jnp.einsum('rbej,rbjc->rbec', select, key_blocks, preferred_element_type=...]
    dot_general x4 -> x7, matrix products: 9.63 us -> 7.36 us  [the longest x1 2.83 us: shards(): jnp.einsum('rbej,rhbj->rhbe', chosen, decay_blocks, precision=HIGHEST)]
  transfers between devices with their start and end apart: 2 -> 1, of which waited for: 0 -> 0; matrix products, arithmetic and copies ran while one was open for 31% -> 14% of each run, Pallas kernels for 0% -> 0%
where the time goes in v1:
time: 157 us; the launch traced here: 155 us
  blocking collectives  105 us (67%)
  local copies, waits for them, and re-layouts  18.8 us (12%)
  other arithmetic  11.5 us (7%)
  starting transfers between devices  10.1 us (6%)
  matrix products  8.72 us (6%)
    all_gather x1, blocking collectives, shards(): totals = lax.all_gather(own_total, 'seq')  70.1 us
    all_gather x1, blocking collectives, shards(): every = lax.all_gather(stats, 'seq')  15.4 us
    all_gather x1, blocking collectives, shards(): arrived = lax.all_gather(packed_fresh, 'grp', axis=0, tiled=True)  10.3 us
    all_to_all x1, starting transfers between devices, shards(): lax.all_to_all(jnp.stack([packed_keys, packed_values]), 'seq', split_axis...  10.1 us
    psum x1, blocking collectives, shards(): layer_out = lax.psum(partial_out, 'head').astype(bf16)  9.03 us
    unnamed x40, local copies, waits for them, and re-layouts  5.05 us
  transfers between devices with their start and end apart: 1, of which 0 were waited for; matrix products, arithmetic and copies ran while one was open for 14% of the time, Pallas kernels for 0%

profile of v1, /device:TPU:1, one launch (start us, length us, event | category | flops | bytes accessed | tf_op | source)
XLA Modules:
  0.0 155.1 jit_solution(16878182813551151916)
XLA Ops:
  0.6 0.9 broadcast_compare_fusion.2
  1.5 0.8 convert_element_type.92
  2.3 0.7 broadcast_select_fusion.4
  3.1 0.8 reshape.315
  4.3 1.3 broadcast_compare_fusion.3
  6.2 0.7 convolution_convert_fusion
  7.0 1.7 %copy-done.4 = bf16[8,512,384]{2,1,0:T(8,128)(2,1)S(1)} copy-done((bf16[8,512,384]{2,1,0:T(8,128)(2,1)S(1)}, bf16[8,512,384]{2,1,0:T(8,128)(2,1)}, u32[]{:S(2)}) %copy-start.4) | copy-done | bytes 3145752
  8.6 0.7 convolution_convert_fusion.1
  9.3 0.9 copy.48
  10.4 0.9 copy.49
  11.4 2.1 %pad_maximum_fusion = bf16[2,8,256,384]{3,1,0,2:T(8,128)(2,1)} fusion(bf16[1,8,256,384]{3,1,0,2:T(8,128)(2,1)S(1)} %copy.49, bf16[1,8,256,384]{3,1,0,2:T(8,128)(2,1)S(1)} %copy.48), kind=kLoop, calls=%fused_computation.1 | loop fusion | flops 1572864 | bytes 6291456 | tf_op jit(solution)/shard_map/stack | solution.py:91
  13.5 10.1 %all-to-all-start = ((bf16[2,8,256,384]{3,1,0,2:T(8,128)(2,1)}), bf16[2,8,256,384]{3,1,0,2:T(8,128)(2,1)}, u32[]{:S(2)}, u32[]{:S(2)}) async-start(bf16[2,8,256,384]{3,1,0,2:T(8,128)(2,1)} %pad_maximum_fusion), calls=%async_computation | async-start | bytes 6291456 | tf_op jit(solution)/shard_map/all_to_all | solution.py:90
  23.7 10.3 %all_gather.17 = bf16[32,1158]{1,0:T(8,128)(2,1)S(1)} all-gather(bf16[8,1158]{1,0:T(8,128)(2,1)S(1)} %pad_maximum_fusion.5), channel_id=1, replica_groups=mesh['grp'=4,'seq'=16,'head'=4] {'grp'}, dimensions={0}, use_global_device_ids=true | all-gather | bytes 92640 | tf_op jit(solution)/shard_map/all_gather | solution.py:30
  35.6 70.1 %all-gather = f32[128,6]{1,0:T(8,128)S(1)} all-gather(f32[8,6]{1,0:T(8,128)S(1)} %copy.52), channel_id=2, replica_groups=mesh['grp'=4,'seq'=16,'head'=4] {'seq'}, dimensions={0}, use_global_device_ids=true | all-gather | bytes 3264 | tf_op jit(solution)/shard_map/all_gather | solution.py:50
  106.8 0.7 reduce_sum.107
  107.8 0.8 fusion.33
  108.5 1.0 select_reduce_fusion.1
  111.4 2.8 %fusion.5 = f32[8,6,8,31]{3,1,2,0:T(8,128)S(1)} fusion(f32[8,8]{1,0:T(8,128)S(1)} %copy-done.10, s32[8,8,64]{2,1,0:T(8,128)S(1)} %fusion.12, pred[8,8,64]{2,1,0:T(8,128)(4,1)S(1)} %eq.81, f32[8,6,8,64]{3,2,1,0:T(8,128)} %copy-done.5, f32[8,8,31]{2,1,0:T(8,128)S(1)} %subtract_multiply_fusion), kind=kOutput, calls=%fused_computation.11 | convolution fusion | flops 9535104 | bytes 174592 | tf_op jit(solution)/shard_map/rbej,rhbj->rhbe/dot_general | solution.py:94
  115.3 2.0 %fusion.51 = (f32[8,6]{1,0:T(8,128)S(1)}, f32[8,6,256]{2,1,0:T(8,128)S(1)}) fusion(f32[8,6,256]{2,0,1:T(8,128)S(1)} %reshape.319, bf16[8,256,384]{2,1,0:T(8,128)(2,1)} %bitcast.50, pred[384,6]{0,1:T(8,128)(4,1)S(1)} %iota_compare_fusion.4, bf16[8,384]{1,0:T(8,128)(2,1)S(1)} %copy-done.12), kind=kOutput, calls=%fused_computation.102 | convolution fusion | flops 9492432 | bytes 1679808 | tf_op jit(solution)/shard_map/rnc,rch->rhn/dot_general | solution.py:112
  117.9 15.4 %all-gather.1 = f32[128,396]{1,0:T(8,128)S(1)} all-gather(f32[8,396]{1,0:T(8,128)S(1)} %pad_maximum_fusion.6), channel_id=3, replica_groups=mesh['grp'=4,'seq'=16,'head'=4] {'seq'}, dimensions={0}, use_global_device_ids=true | all-gather | bytes 215424 | tf_op jit(solution)/shard_map/all_gather | solution.py:121
  133.4 0.7 multiply_add_fusion
  134.2 0.7 reshape.327
  134.9 0.7 reshape.324
  135.7 0.7 reshape.326
  136.4 1.0 broadcast_in_dim.169
  137.4 1.9 %reshape.325 = f32[16,8,384]{2,1,0:T(8,128)} reshape(f32[16,8,6,64]{3,2,1,0:T(8,128)} %broadcast_in_dim.169) | data formatting | bytes 393216 | tf_op jit(solution)/shard_map/reshape | solution.py:128
  139.2 1.0 fusion.20
  140.3 0.9 fusion.35
  141.1 9.0 %psum.7 = bf16[8,96]{1,0:T(8,128)(2,1)} all-reduce(f32[8,96]{1,0:T(8,128)S(1)} %fusion.35), channel_id=1, replica_groups=mesh['grp'=4,'seq'=16,'head'=4] {'head'}, use_global_device_ids=true, to_apply=%region_14.15 | all-reduce | flops 768 | bytes 4608 | tf_op jit(solution)/shard_map/psum | solution.py:148
  150.2 2.2 %slice_bitcast_fusion = (bf16[8,256,384]{2,0,1:T(8,128)(2,1)S(1)}, bf16[8,256,384]{2,0,1:T(8,128)(2,1)S(1)}) fusion(bf16[2,8,256,384]{3,1,0,2:T(8,128)(2,1)} %all-to-all-done), kind=kLoop, calls=%fused_computation.8 | loop fusion | bytes 6291456 | tf_op jit(solution)/shard_map/squeeze | solution.py:149
  152.4 1.3 copy.61
  153.7 1.3 copy.60
  (88 shorter events, 8.0 us)
Async XLA Ops:
  0.6 5.6 %copy-start = (bf16[8,512,384]{2,1,0:T(8,128)(2,1)S(1)}, bf16[8,512,384]{2,1,0:T(8,128)(2,1)}, u32[]{:S(2)}) copy-start(bf16[8,512,384]{2,1,0:T(8,128)(2,1)} %param.11) | copy-start | bytes 9437188
  5.6 1.3 copy-start.9
  5.7 1.2 copy-start.11
  6.2 2.4 %copy-start.4 = (bf16[8,512,384]{2,1,0:T(8,128)(2,1)S(1)}, bf16[8,512,384]{2,1,0:T(8,128)(2,1)}, u32[]{:S(2)}) copy-start(bf16[8,512,384]{2,1,0:T(8,128)(2,1)} %param.10) | copy-start | bytes 9437188
  7.0 3.5 %copy-start.1 = (bf16[8,8,32,384]{3,2,1,0:T(8,128)(2,1)}, bf16[8,8,32,384]{3,2,1,0:T(8,128)(2,1)S(1)}, u32[]{:S(2)}) copy-start(bf16[8,8,32,384]{3,2,1,0:T(8,128)(2,1)S(1)} %convolution_convert_fusion) | copy-start | bytes 4718596
  9.3 1.1 copy-start.3
  13.5 10.2 %copy-start.18 = (s32[8]{0:T(128)S(1)}, s32[8]{0:T(128)}, u32[]{:S(2)}) copy-start(s32[8]{0:T(128)} %param.16) | copy-start | bytes 100
  13.5 10.2 %copy-start.13 = (bf16[3,8,384]{2,1,0:T(8,128)(2,1)S(1)}, bf16[3,8,384]{2,1,0:T(8,128)(2,1)}, u32[]{:S(2)}) copy-start(bf16[3,8,384]{2,1,0:T(8,128)(2,1)} %param.17) | copy-start | bytes 55300
  13.5 10.2 %copy-start.16 = (bf16[8,6]{1,0:T(8,128)(2,1)S(1)}, bf16[8,6]{1,0:T(8,128)(2,1)}, u32[]{:S(2)}) copy-start(bf16[8,6]{1,0:T(8,128)(2,1)} %param.18) | copy-start | bytes 292
  13.5 21.9 %copy-start.17 = (s32[8]{0:T(128)S(1)}, s32[8]{0:T(128)}, u32[]{:S(2)}) copy-start(s32[8]{0:T(128)} %param.15) | copy-start | bytes 100
  13.5 22.0 %copy-start.7 = (f32[8,6,512]{2,0,1:T(8,128)S(1)}, f32[8,6,512]{2,0,1:T(8,128)}, u32[]{:S(2)}) copy-start(f32[8,6,512]{2,0,1:T(8,128)} %param.12) | copy-start | bytes 294916
  13.5 136.7 %all-to-all-start = ((bf16[2,8,256,384]{3,1,0,2:T(8,128)(2,1)}), bf16[2,8,256,384]{3,1,0,2:T(8,128)(2,1)}, u32[]{:S(2)}, u32[]{:S(2)}) async-start(bf16[2,8,256,384]{3,1,0,2:T(8,128)(2,1)} %pad_maximum_fusion), calls=%async_computation | async-start | bytes 6291456 | tf_op jit(solution)/shard_map/all_to_all | solution.py:90
  34.7 0.6 copy-start.6
  107.5 3.2 %copy-start.10 = (f32[8,8]{1,0:T(8,128)S(1)}, f32[8,8]{1,0:T(8,128)}, u32[]{:S(2)}) copy-start(f32[8,8]{1,0:T(8,128)} %copy-done.9) | copy-start | bytes 772
  107.5 3.8 %copy-start.15 = (pred[8,8]{1,0:T(8,128)(4,1)S(1)}, pred[8,8]{1,0:T(8,128)(4,1)}, u32[]{:S(2)}) copy-start(pred[8,8]{1,0:T(8,128)(4,1)} %get-tuple-element.31) | copy-start | bytes 196
  109.5 0.7 copy-start.5
  111.3 4.0 %copy-start.12 = (bf16[8,384]{1,0:T(8,128)(2,1)S(1)}, bf16[8,384]{1,0:T(8,128)(2,1)}, u32[]{:S(2)}) copy-start(bf16[8,384]{1,0:T(8,128)(2,1)} %slice.40) | copy-start | bytes 18436
  114.6 2.9 %copy-start.2 = (bf16[8,8,32,384]{3,2,1,0:T(8,128)(2,1)S(1)}, bf16[8,8,32,384]{3,2,1,0:T(8,128)(2,1)}, u32[]{:S(2)}) copy-start(bf16[8,8,32,384]{3,2,1,0:T(8,128)(2,1)} %copy-done.1) | copy-start | bytes 4718596
  117.2 16.2 %copy-start.14 = (f32[8,6]{1,0:T(8,128)S(1)}, f32[8,6]{1,0:T(8,128)}, u32[]{:S(2)}) copy-start(f32[8,6]{1,0:T(8,128)} %reduce_sum.107) | copy-start | bytes 580
  136.4 3.9 %copy-start.8 = (bf16[384,96]{0,1:T(8,128)(2,1)S(1)}, bf16[384,96]{0,1:T(8,128)(2,1)}, u32[]{:S(2)}) copy-start(bf16[384,96]{0,1:T(8,128)(2,1)} %param.19) | copy-start | bytes 221188
